TPU v7x, 32 devices: a whole 2x2x4 slice. The times are simulated.
32 devices in a mesh: energy: 2 (over y), slab: 4 (over z), orb: 2 (over x), rhs: 2 (over core).
Axes of the slice: x: 2, y: 2, z: 4, core: 2. Of those that a mesh axis runs over, the one named last changes fastest.
Arguments:
- diag_blocks: float32 [16, 192, 384], P(('energy', 'slab'), 'orb'), parts along dimension 0, may hold values from -8 to 8, as said below
- couplings: float32 [16, 192, 384], P(('energy', 'slab')), parts along dimension 0, may hold values from -8 to 8
- sources: float32 [16, 32, 384], P(('energy', 'slab'), ('orb', 'rhs')), parts along dimension 0, may hold values from -8 to 8
Outputs:
- solution: float32 [16, 32, 384], P(('energy', 'slab'), ('orb', 'rhs')), parts along dimension 0
There are 2 independent parts, one for each index of `energy`. A program takes and returns all parts, laid end to end along the dimension named above; each array names one. Nothing has to cross between parts.
Inputs may be any that keep to these rules, and one draw needn't show every extreme that they name: Every diag_blocks[n] is Hermitian, and together with couplings it makes K positive definite with smallest eigenvalue 0.01 or more.
All inputs are finite; a program needn't handle non-finite values.
Results may differ from a plain program's by a relative error of at most 0.0003.
Values sent between devices are 32-bit elements; how exact they have to be, the bound alone decides.
A program may use at most 128 MiB of HBM per device.

v0:
```python
import jax
import jax.numpy as jnp
from jax import lax
from jax.sharding import PartitionSpec as P


def partner_2(shard, axis, distance):
    return lax.ppermute(shard, axis, [(i, i ^ 1 << distance) for i in range(lax.axis_size(axis))])


def embed(columns):
    block_order = columns.shape[1] // 2
    turned = jnp.concatenate([-columns[:, block_order:], columns[:, :block_order]], axis=1)
    return jnp.concatenate([columns, turned], axis=0)


def times(left, right):
    return jnp.dot(left, right, precision=lax.Precision.HIGHEST, preferred_element_type=jnp.float32)


def times_flipped(left, right):
    return lax.dot_general(
        left,
        right,
        (((1,), (1,)), ((), ())),
        precision=lax.Precision.HIGHEST,
        preferred_element_type=jnp.float32,
    )


def inner_product(left, right):
    return lax.dot_general(
        left,
        right,
        (((0,), (0,)), ((), ())),
        precision=lax.Precision.HIGHEST,
        preferred_element_type=jnp.float32,
    )


def apply_inverse(factor, rows):
    return jax.scipy.linalg.cho_solve((factor, True), rows.T).T


def chain_solve(loads, factors):
    length = len(loads)
    lowered = [loads[0]]
    results = [None] * length
    results[length - 1] = apply_inverse(factors[length - 1], lowered[length - 1])
    return results


def choose_sides(is_lower, mine, theirs):
    first_side = jnp.where(is_lower, mine, theirs)
    second_side = jnp.where(is_lower, theirs, mine)
    return (first_side, second_side)


def local(diag_blocks, couplings, sources):
    layer_count = diag_blocks.shape[0]
    narrow = diag_blocks.shape[1]
    block_order = diag_blocks.shape[2] // 2
    slab_index = lax.axis_index("slab")
    col_start = lax.axis_index("orb") * narrow
    first_coupling = couplings[0] * (slab_index > 0).astype(jnp.float32)
    coupling_list = [first_coupling] + [couplings[1]]
    embeds = [embed(block) for block in coupling_list]
    interior = layer_count - 1
    pivot_local = diag_blocks[0]
    pivot_whole = lax.all_gather(pivot_local, "orb", axis=0, tiled=True)
    factors = [jnp.linalg.cholesky(embed(pivot_whole))]
    spike_upper = lax.dynamic_slice_in_dim(first_coupling, col_start, narrow, 0)
    spike_lower = lax.dynamic_slice_in_dim(
        embeds[layer_count - 1][:, :block_order], col_start, narrow, 1
    ).T
    chain_loads = [jnp.concatenate([spike_upper, spike_lower, sources[0]], axis=0)]
    solved = chain_solve(chain_loads, factors)
    top_rows = solved[0]
    bottom_rows = solved[interior - 1]
    upper_upper = -times_flipped(top_rows[:narrow], embeds[0])
    upper_lower = -times_flipped(top_rows[narrow : 2 * narrow], embeds[0])
    lower_lower = diag_blocks[layer_count - 1] - times(
        bottom_rows[narrow : 2 * narrow], embeds[layer_count - 1]
    )
    load_upper = -times_flipped(top_rows[2 * narrow :], embeds[0])
    load_lower = sources[layer_count - 1] - times(
        bottom_rows[2 * narrow :], embeds[layer_count - 1]
    )
    upper_upper, upper_lower, lower_lower = (
        lax.all_gather(upper_upper, "orb", axis=0, tiled=True),
        lax.all_gather(upper_lower, "orb", axis=0, tiled=True),
        lax.all_gather(lower_lower, "orb", axis=0, tiled=True),
    )
    level_count = lax.axis_size("slab").bit_length() - 1
    stored = []
    for level_index in range(level_count):
        is_lower = slab_index // 2**level_index % 2 == 0
        partner = partner_2(
            (upper_upper, upper_lower, lower_lower, load_upper, load_lower), "slab", level_index
        )
        first_uu, second_uu = choose_sides(is_lower, upper_upper, partner[0])
        first_uv, second_uv = choose_sides(is_lower, upper_lower, partner[1])
        first_vv, second_vv = choose_sides(is_lower, lower_lower, partner[2])
        first_gu, second_gu = choose_sides(is_lower, load_upper, partner[3])
        first_gv, second_gv = choose_sides(is_lower, load_lower, partner[4])
        pivot_part = first_vv + second_uu
        shared_load = first_gv + second_gu
        pivot_whole, first_cross, second_cross = (pivot_part, first_uv, second_uv)
        factor = jnp.linalg.cholesky(embed(pivot_whole))
        first_embed = embed(first_cross)
        second_embed = embed(second_cross)
        weight_first = jax.scipy.linalg.solve_triangular(factor, first_embed, lower=True)
        weight_second = jax.scipy.linalg.solve_triangular(factor, second_embed.T, lower=True)
        upper_upper = first_uu - inner_product(weight_first[:, :block_order], weight_first)
        upper_lower = -inner_product(weight_second[:, :block_order], weight_first)
        lower_lower = second_vv - inner_product(weight_second[:, :block_order], weight_second)
        solved_load = apply_inverse(factor, shared_load)
        load_upper = first_gu - times(solved_load, first_embed)
        load_lower = second_gv - times_flipped(solved_load, second_embed)
        stored.append((factor, first_embed, second_embed, shared_load, is_lower))
    final_factor = jnp.linalg.cholesky(embed(lower_lower))
    value_lower = apply_inverse(final_factor, load_lower)
    value_upper = jnp.zeros_like(load_lower)
    for factor, first_embed, second_embed, shared_load, is_lower in reversed(stored):
        remaining = (
            shared_load - times_flipped(value_upper, first_embed) - times(value_lower, second_embed)
        )
        middle = apply_inverse(factor, remaining)
        value_upper, value_lower = (
            jnp.where(is_lower, value_upper, middle),
            jnp.where(is_lower, middle, value_lower),
        )
    final_loads = [sources[0]]
    final_loads[0] = final_loads[0] - times(value_upper, embeds[0])
    final_loads[interior - 1] = final_loads[interior - 1] - times_flipped(
        value_lower, embeds[layer_count - 1]
    )
    interior_values = chain_solve(final_loads, factors)
    return jnp.stack(interior_values + [value_lower], axis=0)


def solution(mesh):
    placed = (
        P(("energy", "slab"), "orb", None),
        P(("energy", "slab"), None, None),
        P(("energy", "slab"), ("orb", "rhs"), None),
    )
    return jax.shard_map(
        local,
        mesh=mesh,
        in_specs=placed,
        out_specs=P(("energy", "slab"), ("orb", "rhs"), None),
        check_vma=False,
    )
```

profile of v0, /device:TPU:0, one launch (start us, length us, event | category | flops | bytes accessed | tf_op | source)
XLA Modules:
  0.0 541.4 jit_solution(309252901826706414)
XLA Ops:
  9.4 11.7 %cholesky.338 = f32[128,128]{1,0:T(8,128)S(1)} custom-call(f32[128,128]{1,0:T(8,128)S(1)} %cholesky.546), custom_call_target="Cholesky" | custom-call | tf_op jit(solution)/shard_map/jit(cholesky)/cholesky | solution.py:71
  21.1 9.8 %custom-call.43 = f32[1,128,128]{1,2,0:T(8,128)S(1)} custom-call(f32[1,128,128]{2,1,0:T(8,128)S(1)} %get-tuple-element.176), custom_call_target="InvertDiagBlocksLowerTriangular" | custom-call | tf_op jit(solution)/shard_map/jit(cholesky)/cholesky | solution.py:71
  31.6 11.7 %cholesky.357 = f32[128,128]{1,0:T(8,128)S(1)} custom-call(f32[128,128]{1,0:T(8,128)S(1)} %cholesky.550), custom_call_target="Cholesky" | custom-call | tf_op jit(solution)/shard_map/jit(cholesky)/cholesky | solution.py:71
  43.3 9.9 %custom-call.44 = f32[1,128,128]{1,2,0:T(8,128)S(1)} custom-call(f32[1,128,128]{2,1,0:T(8,128)S(1)} %get-tuple-element.173), custom_call_target="InvertDiagBlocksLowerTriangular" | custom-call | tf_op jit(solution)/shard_map/jit(cholesky)/cholesky | solution.py:71
  53.8 11.7 %cholesky.376 = f32[128,128]{1,0:T(8,128)S(1)} custom-call(f32[128,128]{1,0:T(8,128)S(1)} %convolution_subtract_fusion.12), custom_call_target="Cholesky" | custom-call | tf_op jit(solution)/shard_map/jit(cholesky)/cholesky | solution.py:71
  74.6 29.5 %custom-call.59 = f32[3,128,128]{1,2,0:T(8,128)S(1)} custom-call(f32[3,128,128]{2,1,0:T(8,128)S(1)} %get-tuple-element.82), custom_call_target="InvertDiagBlocksLowerTriangular" | custom-call | tf_op jit(solution)/shard_map/jit(_cho_solve)/triangular_solve | solution.py:42
  140.7 11.7 %cholesky.391 = f32[128,128]{1,0:T(8,128)S(1)} custom-call(f32[128,128]{1,0:T(8,128)S(1)} %cholesky.554), custom_call_target="Cholesky" | custom-call | tf_op jit(solution)/shard_map/jit(cholesky)/cholesky | solution.py:109
  152.5 9.8 %custom-call.45 = f32[1,128,128]{1,2,0:T(8,128)S(1)} custom-call(f32[1,128,128]{2,1,0:T(8,128)S(1)} %get-tuple-element.169), custom_call_target="InvertDiagBlocksLowerTriangular" | custom-call | tf_op jit(solution)/shard_map/jit(cholesky)/cholesky | solution.py:109
  162.9 11.7 %cholesky.410 = f32[128,128]{1,0:T(8,128)S(1)} custom-call(f32[128,128]{1,0:T(8,128)S(1)} %cholesky.558), custom_call_target="Cholesky" | custom-call | tf_op jit(solution)/shard_map/jit(cholesky)/cholesky | solution.py:109
  176.0 10.2 %custom-call.46 = f32[1,128,128]{1,2,0:T(8,128)S(1)} custom-call(f32[1,128,128]{2,1,0:T(8,128)S(1)} %get-tuple-element.166), custom_call_target="InvertDiagBlocksLowerTriangular" | custom-call | tf_op jit(solution)/shard_map/jit(cholesky)/cholesky | solution.py:109
  186.6 11.7 %cholesky.429 = f32[128,128]{1,0:T(8,128)S(1)} custom-call(f32[128,128]{1,0:T(8,128)S(1)} %convolution_subtract_fusion.11), custom_call_target="Cholesky" | custom-call | tf_op jit(solution)/shard_map/jit(cholesky)/cholesky | solution.py:109
  207.1 29.7 %custom-call.47 = f32[3,128,128]{1,2,0:T(8,128)S(1)} custom-call(f32[3,128,128]{2,1,0:T(8,128)S(1)} %get-tuple-element.74), custom_call_target="InvertDiagBlocksLowerTriangular" | custom-call | tf_op jit(solution)/shard_map/jit(_solve_triangular)/triangular_solve | solution.py:113
  261.6 22.3 %collective-permute-done.4 = f32[192,384]{0,1:T(8,128)S(1)} collective-permute-done((f32[192,384]{0,1:T(8,128)S(1)}, f32[192,384]{0,1:T(8,128)S(1)}, u32[]{:S(2)}, u32[]{:S(2)}) %collective-permute-start.4) | collective-permute-done | bytes 294944 | tf_op jit(solution)/shard_map/ppermute | solution.py:8
  296.5 12.1 %cholesky.444 = f32[128,128]{1,0:T(8,128)S(1)} custom-call(f32[128,128]{1,0:T(8,128)S(1)} %cholesky.562), custom_call_target="Cholesky" | custom-call | tf_op jit(solution)/shard_map/jit(cholesky)/cholesky | solution.py:109
  309.2 9.8 %custom-call.49 = f32[1,128,128]{1,2,0:T(8,128)S(1)} custom-call(f32[1,128,128]{2,1,0:T(8,128)S(1)} %get-tuple-element.162), custom_call_target="InvertDiagBlocksLowerTriangular" | custom-call | tf_op jit(solution)/shard_map/jit(cholesky)/cholesky | solution.py:109
  319.6 12.3 %cholesky.463 = f32[128,128]{1,0:T(8,128)} custom-call(f32[128,128]{1,0:T(8,128)S(1)} %cholesky.566), custom_call_target="Cholesky" | custom-call | tf_op jit(solution)/shard_map/jit(cholesky)/cholesky | solution.py:109
  334.8 10.4 %custom-call.50 = f32[1,128,128]{1,2,0:T(8,128)} custom-call(f32[1,128,128]{2,1,0:T(8,128)S(1)} %get-tuple-element.159), custom_call_target="InvertDiagBlocksLowerTriangular" | custom-call | tf_op jit(solution)/shard_map/jit(cholesky)/cholesky | solution.py:109
  346.6 11.9 %cholesky.482 = f32[128,128]{1,0:T(8,128)S(1)} custom-call(f32[128,128]{1,0:T(8,128)S(1)} %convolution_subtract_fusion.10), custom_call_target="Cholesky" | custom-call | tf_op jit(solution)/shard_map/jit(cholesky)/cholesky | solution.py:109
  367.3 29.5 %custom-call.57 = f32[3,128,128]{1,2,0:T(8,128)S(1)} custom-call(f32[3,128,128]{2,1,0:T(8,128)S(1)} %get-tuple-element.80), custom_call_target="InvertDiagBlocksLowerTriangular" | custom-call | tf_op jit(solution)/shard_map/jit(_cho_solve)/triangular_solve | solution.py:42
  412.7 11.7 %cholesky.497 = f32[128,128]{1,0:T(8,128)S(1)} custom-call(f32[128,128]{1,0:T(8,128)S(1)} %cholesky.570), custom_call_target="Cholesky" | custom-call | tf_op jit(solution)/shard_map/jit(cholesky)/cholesky | solution.py:121
  438.2 11.9 %cholesky.516 = f32[128,128]{1,0:T(8,128)S(1)} custom-call(f32[128,128]{1,0:T(8,128)S(1)} %cholesky.574), custom_call_target="Cholesky" | custom-call | tf_op jit(solution)/shard_map/jit(cholesky)/cholesky | solution.py:121
  464.0 11.7 %cholesky.535 = f32[128,128]{1,0:T(8,128)S(1)} custom-call(f32[128,128]{1,0:T(8,128)S(1)} %convolution_subtract_fusion.9), custom_call_target="Cholesky" | custom-call | tf_op jit(solution)/shard_map/jit(cholesky)/cholesky | solution.py:121
  481.7 10.7 %while.20 = (s32[]{:T(128)}, f32[384,384]{1,0:T(8,128)}, s32[3,2]{0,1:T(2,128)S(1)}, f32[3,128,128]{2,1,0:T(8,128)}, s32[]{:T(128)}) while((s32[]{:T(128)}, f32[384,384]{1,0:T(8,128)}, s32[3,2]{0,1:T(2,128)S(1)}, f32[3,128,128]{2,1,0:T(8,128)}, s32[]{:T(128)}) %tuple.132), condition=%wide.while_cond.1.clone.1, body=%wide.while_body.1.clone.1.sunk | while | flops 2 | bytes 132705 | solution.py:42
  492.4 31.1 %custom-call.56 = f32[3,128,128]{1,2,0:T(8,128)} custom-call(f32[3,128,128]{2,1,0:T(8,128)} %get-tuple-element.79), custom_call_target="InvertDiagBlocksLowerTriangular" | custom-call | tf_op jit(solution)/shard_map/jit(_cho_solve)/triangular_solve | solution.py:42
  (403 shorter events, 205.9 us)
Async XLA Ops:
  68.7 35.5 %copy-start.44 = (f32[2,192,384]{2,1,0:T(8,128)S(1)}, f32[2,192,384]{2,1,0:T(8,128)}, u32[]{:S(2)}) copy-start(f32[2,192,384]{2,1,0:T(8,128)} %param.9) | copy-start | bytes 1769476
  74.6 34.1 %copy-start = (f32[384,384]{1,0:T(8,128)}, f32[384,384]{1,0:T(8,128)S(1)}, u32[]{:S(2)}) copy-start(f32[384,384]{1,0:T(8,128)S(1)} %get-tuple-element.365) | copy-start | bytes 1769476
  104.3 17.2 %copy-start.8 = (f32[192,192]{1,0:T(8,128)}, f32[192,192]{1,0:T(8,128)S(1)}, u32[]{:S(2)}) copy-start(f32[192,192]{1,0:T(8,128)S(1)} %get-tuple-element.147) | copy-start | bytes 442372
  104.4 17.2 %copy-start.10 = (f32[192,192]{1,0:T(8,128)}, f32[192,192]{1,0:T(8,128)S(1)}, u32[]{:S(2)}) copy-start(f32[192,192]{1,0:T(8,128)S(1)} %get-tuple-element.148) | copy-start | bytes 442372
  109.9 28.0 %copy-start.49 = (f32[8,384]{1,0:T(8,128)}, f32[8,384]{1,0:T(8,128)S(1)}, u32[]{:S(2)}) copy-start(f32[8,384]{1,0:T(8,128)S(1)} %convolution_subtract_fusion.17) | copy-start | bytes 36868
  109.9 28.0 %collective-permute-start.5 = (f32[8,384]{1,0:T(8,128)S(1)}, f32[8,384]{1,0:T(8,128)S(1)}, u32[]{:S(2)}, u32[]{:S(2)}) collective-permute-start(f32[8,384]{1,0:T(8,128)S(1)} %convolution_subtract_fusion.17), channel_id=1, source_target_pairs={{0,4},{4,0},{8,12},{12,8},{1,5},{5,1},{9,13},{13,9},{2,6},{6,2},{1... | collective-permute-start | bytes 36872 | tf_op jit(solution)/shard_map/ppermute | solution.py:8
  112.0 16.9 %copy-start.27 = (f32[192,192]{1,0:T(8,128)}, f32[192,192]{1,0:T(8,128)S(1)}, u32[]{:S(2)}) copy-start(f32[192,192]{1,0:T(8,128)S(1)} %get-tuple-element.145) | copy-start | bytes 442372
  112.0 16.9 %copy-start.29 = (f32[192,192]{1,0:T(8,128)}, f32[192,192]{1,0:T(8,128)S(1)}, u32[]{:S(2)}) copy-start(f32[192,192]{1,0:T(8,128)S(1)} %get-tuple-element.146) | copy-start | bytes 442372
  112.6 25.3 %copy-start.51 = (f32[8,384]{1,0:T(8,128)}, f32[8,384]{1,0:T(8,128)S(1)}, u32[]{:S(2)}) copy-start(f32[8,384]{1,0:T(8,128)S(1)} %convolution_negate_fusion.3) | copy-start | bytes 36868
  112.6 25.3 %collective-permute-start.6 = (f32[8,384]{1,0:T(8,128)S(1)}, f32[8,384]{1,0:T(8,128)S(1)}, u32[]{:S(2)}, u32[]{:S(2)}) collective-permute-start(f32[8,384]{1,0:T(8,128)S(1)} %convolution_negate_fusion.3), channel_id=1, source_target_pairs={{0,4},{4,0},{8,12},{12,8},{1,5},{5,1},{9,13},{13,9},{2,6},{6,2},{1... | collective-permute-start | bytes 36872 | tf_op jit(solution)/shard_map/ppermute | solution.py:8
  119.6 18.9 %collective-permute-start.1 = (f32[192,384]{0,1:T(8,128)S(1)}, f32[192,384]{0,1:T(8,128)S(1)}, u32[]{:S(2)}, u32[]{:S(2)}) collective-permute-start(f32[192,384]{0,1:T(8,128)S(1)} %copy.27), channel_id=1, source_target_pairs={{0,4},{4,0},{8,12},{12,8},{1,5},{5,1},{9,13},{13,9},{2,6},{6,2},{1... | collective-permute-start | bytes 884744 | tf_op jit(solution)/shard_map/ppermute | solution.py:8
  128.1 11.2 %collective-permute-start = (f32[192,384]{0,1:T(8,128)S(1)}, f32[192,384]{0,1:T(8,128)S(1)}, u32[]{:S(2)}, u32[]{:S(2)}) collective-permute-start(f32[192,384]{0,1:T(8,128)S(1)} %copy.24), channel_id=1, source_target_pairs={{0,4},{4,0},{8,12},{12,8},{1,5},{5,1},{9,13},{13,9},{2,6},{6,2},{1... | collective-permute-start | bytes 884744 | tf_op jit(solution)/shard_map/ppermute | solution.py:8
  136.6 100.2 %collective-permute-start.2 = (f32[192,384]{0,1:T(8,128)}, f32[192,384]{0,1:T(8,128)}, u32[]{:S(2)}, u32[]{:S(2)}) collective-permute-start(f32[192,384]{0,1:T(8,128)} %copy.30), channel_id=1, source_target_pairs={{0,4},{4,0},{8,12},{12,8},{1,5},{5,1},{9,13},{13,9},{2,6},{6,2},{1... | collective-permute-start | bytes 884744 | tf_op jit(solution)/shard_map/ppermute | solution.py:8
  241.5 19.4 %collective-permute-start.8 = (f32[8,384]{1,0:T(8,128)S(1)}, f32[8,384]{1,0:T(8,128)S(1)}, u32[]{:S(2)}, u32[]{:S(2)}) collective-permute-start(f32[8,384]{1,0:T(8,128)S(1)} %select_subtract_fusion.3), channel_id=1, source_target_pairs={{0,8},{4,12},{8,0},{12,4},{1,9},{5,13},{9,1},{13,5},{2,10},{6,14},... | collective-permute-start | bytes 36872 | tf_op jit(solution)/shard_map/ppermute | solution.py:8
  245.5 15.5 %copy-start.48 = (f32[8,384]{1,0:T(8,128)}, f32[8,384]{1,0:T(8,128)S(1)}, u32[]{:S(2)}) copy-start(f32[8,384]{1,0:T(8,128)S(1)} %select_subtract_fusion.4) | copy-start | bytes 36868
  245.5 15.5 %collective-permute-start.7 = (f32[8,384]{1,0:T(8,128)S(1)}, f32[8,384]{1,0:T(8,128)S(1)}, u32[]{:S(2)}, u32[]{:S(2)}) collective-permute-start(f32[8,384]{1,0:T(8,128)S(1)} %select_subtract_fusion.4), channel_id=1, source_target_pairs={{0,8},{4,12},{8,0},{12,4},{1,9},{5,13},{9,1},{13,5},{2,10},{6,14},... | collective-permute-start | bytes 36872 | tf_op jit(solution)/shard_map/ppermute | solution.py:8
  249.9 34.0 %collective-permute-start.4 = (f32[192,384]{0,1:T(8,128)S(1)}, f32[192,384]{0,1:T(8,128)S(1)}, u32[]{:S(2)}, u32[]{:S(2)}) collective-permute-start(f32[192,384]{0,1:T(8,128)S(1)} %select_subtract_fusion.1), channel_id=1, source_target_pairs={{0,8},{4,12},{8,0},{12,4},{1,9},{5,13},{9,1},{13,5},{2,10},{6,14},... | collective-permute-start | bytes 884744 | tf_op jit(solution)/shard_map/ppermute | solution.py:8
  256.1 36.2 %copy-start.12 = (f32[192,384]{0,1:T(8,128)}, f32[192,384]{0,1:T(8,128)S(1)}, u32[]{:S(2)}) copy-start(f32[192,384]{0,1:T(8,128)S(1)} %select_subtract_fusion.2) | copy-start | bytes 884740
  256.1 36.2 %collective-permute-start.3 = (f32[192,384]{0,1:T(8,128)S(1)}, f32[192,384]{0,1:T(8,128)S(1)}, u32[]{:S(2)}, u32[]{:S(2)}) collective-permute-start(f32[192,384]{0,1:T(8,128)S(1)} %select_subtract_fusion.2), channel_id=1, source_target_pairs={{0,8},{4,12},{8,0},{12,4},{1,9},{5,13},{9,1},{13,5},{2,10},{6,14},... | collective-permute-start | bytes 884744 | tf_op jit(solution)/shard_map/ppermute | solution.py:8
  258.4 141.7 %collective-permute-start.9 = (f32[192,384]{0,1:T(8,128)}, f32[192,384]{0,1:T(8,128)}, u32[]{:S(2)}, u32[]{:S(2)}) collective-permute-start(f32[192,384]{0,1:T(8,128)} %convolution_negate_fusion), channel_id=1, source_target_pairs={{0,8},{4,12},{8,0},{12,4},{1,9},{5,13},{9,1},{13,5},{2,10},{6,14},... | collective-permute-start | bytes 884744 | tf_op jit(solution)/shard_map/ppermute | solution.py:8
  296.4 22.6 %copy-start.35 = (f32[384,384]{1,0:T(8,128)S(1)}, f32[384,384]{1,0:T(8,128)}, u32[]{:S(2)}) copy-start(f32[384,384]{1,0:T(8,128)} %copy-done.34) | copy-start | bytes 1769476
  361.2 35.6 %copy-start.46 = (f32[8,384]{1,0:T(8,128)S(1)}, f32[8,384]{1,0:T(8,128)}, u32[]{:S(2)}) copy-start(f32[8,384]{1,0:T(8,128)} %select_add_fusion.2) | copy-start | bytes 36868
  479.0 44.6 %copy-start.25 = (f32[192,192]{0,1:T(8,128)S(1)}, f32[192,192]{0,1:T(8,128)}, u32[]{:S(2)}) copy-start(f32[192,192]{0,1:T(8,128)} %copy-done.24) | copy-start | bytes 442372
  481.0 42.6 %copy-start.22 = (f32[192,192]{0,1:T(8,128)S(1)}, f32[192,192]{0,1:T(8,128)}, u32[]{:S(2)}) copy-start(f32[192,192]{0,1:T(8,128)} %copy-done.21) | copy-start | bytes 442372
  (50 other events, 74.3 us)
where the time goes:
time: 552 us; the launch traced here: 541 us
  other arithmetic  364 us (66%)
  local copies, waits for them, and re-layouts  50.3 us (9%)
  matrix products  46.1 us (8%)
  waiting for transfers between devices  31.5 us (6%)
  blocking collectives  25.1 us (5%)
  starting transfers between devices  14.8 us (3%)
  between operations  9.34 us (2%)
    another operation x22, other arithmetic, local(): factor = jnp.linalg.cholesky(embed(pivot_whole))  117 us
    another operation x7, other arithmetic, apply_inverse(): return jax.scipy.linalg.cho_solve((factor, True), rows.T).T  92.2 us
    another operation x11, other arithmetic, local(): final_factor = jnp.linalg.cholesky(embed(lower_lower))  58.3 us
    another operation x10, other arithmetic, local(): factors = [jnp.linalg.cholesky(embed(pivot_whole))]  56.3 us
    ppermute x10, waiting for transfers between devices, partner_2(): lax.ppermute(shard, axis, [(i, i ^ 1 << distance) for i in range(lax.axis...  31.5 us
    another operation x2, other arithmetic, local(): jax.scipy.linalg.solve_triangular(factor, second_embed.T, lower=True)  29.7 us
    another operation x32, local copies, waits for them, and re-layouts, apply_inverse(): return jax.scipy.linalg.cho_solve((factor, True), rows.T).T  23.3 us
    another operation x70, matrix products, apply_inverse(): return jax.scipy.linalg.cho_solve((factor, True), rows.T).T  16.7 us
  transfers between devices with their start and end apart: 10, of which 3 were waited for; matrix products, arithmetic and copies ran while one was open for 39% of the time, Pallas kernels for 0%

commit v1 on v0

v1 whole, which is shorter than its diff:
```python
import jax
import jax.numpy as jnp
from jax import lax
from jax.sharding import PartitionSpec as P
from jax.experimental import pallas as pl
from jax.experimental.pallas import tpu as pltpu

HALF = 64
LANES = 2 * HALF


def dot(left, right, dims=((1,), (0,))):
    return lax.dot_general(
        left,
        right,
        (dims, ((), ())),
        precision=lax.Precision.HIGHEST,
        preferred_element_type=jnp.float32,
    )


def dot_flipped(left, right):
    return dot(left, right, ((1,), (1,)))


def lane_sign(shape):
    lane = lax.broadcasted_iota(jnp.int32, shape, 1)
    return jnp.where(lane % LANES < HALF, -1.0, 1.0).astype(jnp.float32)


def times_i(rows):
    pieces = [
        pltpu.roll(rows[:, start : start + LANES], HALF, 1)
        for start in range(0, rows.shape[1], LANES)
    ]
    turned = pieces[0] if len(pieces) == 1 else jnp.concatenate(pieces, axis=1)
    return turned * lane_sign(turned.shape)


def interleave(rows):
    count = rows.shape[1] // LANES
    pieces = []
    for chunk in range(count):
        pieces.append(rows[:, chunk * HALF : (chunk + 1) * HALF])
        pieces.append(rows[:, (count + chunk) * HALF : (count + chunk + 1) * HALF])
    return jnp.concatenate(pieces, axis=1)


def separate(rows):
    count = rows.shape[1] // LANES
    pieces = [rows[:, 2 * chunk * HALF : (2 * chunk + 1) * HALF] for chunk in range(count)]
    pieces += [rows[:, (2 * chunk + 1) * HALF : (2 * chunk + 2) * HALF] for chunk in range(count)]
    return jnp.concatenate(pieces, axis=1)


def embed(rows):
    turned = times_i(rows)
    pieces = []
    for start in range(0, rows.shape[0], HALF):
        pieces += [rows[start : start + HALF], turned[start : start + HALF]]
    return jnp.concatenate(pieces, axis=0)


def compact(embedded):
    return jnp.concatenate(
        [embedded[start : start + HALF] for start in range(0, embedded.shape[0], LANES)], axis=0
    )


GROUP = 8


def invert_group(rows, first, sign, lane, row_id):
    for offset in range(0, GROUP, 2):
        step = first + offset
        at_zero = lane == step
        at_one = lane == step + 1
        at_any = at_zero | at_one | (lane == step + HALF) | (lane == step + 1 + HALF)
        zero_real, zero_imag, one_real, one_imag = (
            jnp.broadcast_to(rows[:, at : at + 1], (GROUP, LANES))
            for at in (step, step + HALF, step + 1, step + 1 + HALF)
        )
        head = zero_real[offset : offset + 1]
        tail = one_real[offset + 1 : offset + 2]
        cross_real = one_real[offset : offset + 1]
        cross_imag = one_imag[offset : offset + 1]
        scale = 1.0 / (head * tail - cross_real * cross_real - cross_imag * cross_imag)
        cleared = jnp.where(at_any, 0.0, rows)
        turned = pltpu.roll(cleared, HALF, 1) * sign
        row_zero = cleared[offset : offset + 1] + jnp.where(at_zero, 1.0, 0.0)
        row_one = cleared[offset + 1 : offset + 2] + jnp.where(at_one, 1.0, 0.0)
        turn_zero = turned[offset : offset + 1] + jnp.where(lane == step + HALF, 1.0, 0.0)
        turn_one = turned[offset + 1 : offset + 2] + jnp.where(lane == step + 1 + HALF, 1.0, 0.0)
        new_zero = (tail * row_zero - cross_real * row_one - cross_imag * turn_one) * scale
        new_one = (head * row_one - cross_real * row_zero + cross_imag * turn_zero) * scale
        spin_zero = (tail * turn_zero - cross_real * turn_one + cross_imag * row_one) * scale
        spin_one = (head * turn_one - cross_real * turn_zero - cross_imag * row_zero) * scale
        fresh = (
            cleared
            - (zero_real * new_zero + zero_imag * spin_zero)
            - (one_real * new_one + one_imag * spin_one)
        )
        rows = jnp.where(
            row_id == offset, new_zero, jnp.where(row_id == offset + 1, new_one, fresh)
        )
    return rows


def invert_small(block):
    lane = lax.broadcasted_iota(jnp.int32, (1, LANES), 1)
    row_id = lax.broadcasted_iota(jnp.int32, (GROUP, 1), 0)
    sign = lane_sign((1, LANES))
    groups = [block[start : start + GROUP] for start in range(0, HALF, GROUP)]
    for home in range(len(groups)):
        first = home * GROUP
        done = invert_group(groups[home], first, sign, lane, row_id)
        spun = pltpu.roll(done, HALF, 1) * sign
        inside = (lane % HALF >= first) & (lane % HALF < first + GROUP)
        for index, group in enumerate(groups):
            if index == home:
                continue
            fresh = jnp.where(inside, 0.0, group)
            for at in range(GROUP):
                fresh = fresh - (
                    group[:, first + at : first + at + 1] * done[at : at + 1]
                    + group[:, first + at + HALF : first + at + HALF + 1] * spun[at : at + 1]
                )
            groups[index] = fresh
        groups[home] = done
    return jnp.concatenate(groups, axis=0)


def invert(ref):
    order = ref.shape[0]

    def step(k, carry):
        rows = pl.ds(pl.multiple_of(k * HALF, HALF), HALF)
        lanes = pl.ds(pl.multiple_of(k * LANES, LANES), LANES)
        small = invert_small(ref[rows, lanes])
        panel = ref[rows, :]
        ref[rows, :] = dot(small, jnp.concatenate([panel, times_i(panel)], axis=0))
        ref[rows, lanes] = small
        fresh = ref[rows, :]
        column = ref[:, lanes]
        ref[:, lanes] = jnp.zeros((order, LANES), jnp.float32)
        ref[...] = ref[...] - dot(column, jnp.concatenate([fresh, times_i(fresh)], axis=0))
        ref[rows, :] = fresh
        return carry

    lax.fori_loop(0, order // HALF, step, 0)


def eliminate(pivot_ref, to_pivot_v, to_pivot_u, block_v, block_u, load_i, load_v, load_u):
    order, rhs = block_v.shape[0], load_i.shape[0]
    invert(pivot_ref)
    inverse = embed(pivot_ref[...])
    stacked = [compact(to_pivot_v), load_i]
    if to_pivot_u is not None:
        stacked.append(compact(to_pivot_u))
    through = dot(jnp.concatenate(stacked, axis=0), inverse)
    toward_v = dot_flipped(through[: order + rhs], to_pivot_v)
    new_v = jnp.concatenate([block_v, load_v], axis=0) - toward_v
    kept = (through[:order], through[order : order + rhs])
    if to_pivot_u is None:
        return new_v, kept
    toward_u = dot_flipped(through, to_pivot_u)
    new_u = jnp.concatenate([block_u, load_u], axis=0) - jnp.concatenate(
        [toward_u[order + rhs :], toward_u[order : order + rhs]], axis=0
    )
    return new_v, new_u, -toward_u[:order], kept + (through[order + rhs :],)


def flip_where(flip, ref, embedded):
    @pl.when(flip)
    def _():
        ref[...] = embedded.T

    @pl.when(jnp.logical_not(flip))
    def _():
        ref[...] = embedded


def is_left():
    return lax.axis_index("slab") < lax.axis_size("slab") // 2


def interior_kernel(diag, inner, outer, loads, new_v, new_u, cross, kept_v, kept_b, kept_u, pivot, to_v, to_u):
    left = is_left()
    order = diag.shape[1]
    at_interior = jnp.where(left, 0, 1)
    flip_where(left, to_v, embed(interleave(inner[...])))
    flip_where(jnp.logical_not(left), to_u, embed(interleave(outer[...])))
    pivot[...] = interleave(diag[at_interior])
    load_i = interleave(loads[at_interior])
    load_v = interleave(loads[1 - at_interior])
    block_v = interleave(diag[1 - at_interior])
    zero = jnp.zeros_like(block_v)
    new_v[...], new_u[...], cross[...], kept = eliminate(
        pivot, to_v[...], to_u[...], block_v, zero, load_i, load_v, jnp.zeros_like(load_v)
    )
    kept_v[...], kept_b[...], kept_u[...] = kept


def level_kernel(own_v, own_u, own_cross, first_v, new_v, kept_v, kept_b, pivot):
    order = pivot.shape[0]
    joined = first_v[...] + own_u[...]
    pivot[...] = joined[:order]
    new_v[...], kept = eliminate(
        pivot, embed(own_cross[...]), None, own_v[:order], None, joined[order:], own_v[order:], None
    )
    kept_v[...], kept_b[...] = kept


def wide_level_kernel(
    own_v, own_u, own_cross, first_v, first_u, first_cross,
    new_v, new_u, cross, kept_v, kept_b, kept_u, pivot,
):
    order = pivot.shape[0]
    joined = first_v[...] + own_u[...]
    pivot[...] = joined[:order]
    new_v[...], new_u[...], cross[...], kept = eliminate(
        pivot,
        embed(own_cross[...]),
        embed(first_cross[...]).T,
        own_v[:order],
        first_u[:order],
        joined[order:],
        own_v[order:],
        first_u[order:],
    )
    kept_v[...], kept_b[...], kept_u[...] = kept


def center_kernel(own, other, coupling, value, pivot, to_other):
    order = pivot.shape[0]
    flip_where(jnp.logical_not(is_left()), to_other, embed(interleave(coupling[...])))
    pivot[...] = other[:order]
    reduced, _ = eliminate(
        pivot, to_other[...], None, own[:order], None, other[order:], own[order:], None
    )
    pivot[...] = reduced[:order]
    invert(pivot)
    value[...] = dot(reduced[order:], embed(pivot[...]))


def back_kernel(value_v, value_u, kept_v, kept_b, kept_u, middle):
    middle[...] = (
        kept_b[...]
        - dot(value_v[...], embed(kept_v[...]))
        - dot(value_u[...], embed(kept_u[...]))
    )


def narrow_back_kernel(value_v, kept_v, kept_b, middle):
    middle[...] = kept_b[...] - dot(value_v[...], embed(kept_v[...]))


def final_kernel(value_v, value_u, kept_v, kept_b, kept_u, result):
    middle = (
        kept_b[...]
        - dot(value_v[...], embed(kept_v[...]))
        - dot(value_u[...], embed(kept_u[...]))
    )
    at_interior = jnp.where(is_left(), 0, 1)
    result[at_interior] = separate(middle)
    result[1 - at_interior] = separate(value_v[...])


def call(kernel, outs, scratch, *operands):
    return pl.pallas_call(
        kernel,
        out_shape=[jax.ShapeDtypeStruct(shape, jnp.float32) for shape in outs],
        scratch_shapes=[pltpu.VMEM(shape, jnp.float32) for shape in scratch],
        compiler_params=pltpu.CompilerParams(vmem_limit_bytes=48 * 1024 * 1024),
    )(*operands)


def gather_columns(shard):
    size = lax.axis_size("orb")
    index = lax.axis_index("orb")
    distance = 1
    while distance < size:
        theirs = lax.ppermute(shard, "orb", [(i, i ^ distance) for i in range(size)])
        first = index // distance % 2 == 0
        shard = jnp.where(
            first,
            jnp.concatenate([shard, theirs], axis=1),
            jnp.concatenate([theirs, shard], axis=1),
        )
        distance *= 2
    return shard


def local(diag_blocks, couplings, sources):
    order, width = couplings.shape[1:]
    rhs = sources.shape[1]
    slabs = lax.axis_size("slab")
    half = slabs // 2
    slab = lax.axis_index("slab")
    left = slab < half
    place = jnp.where(left, slab, slabs - 1 - slab)

    def at(position):
        return (position, slabs - 1 - position)

    shifted = lax.ppermute(couplings[0], "slab", [(i, i - 1) for i in range(half, slabs)])
    diag = gather_columns(diag_blocks)
    outer = jnp.where(left, jnp.where(slab > 0, couplings[0], 0.0), shifted)
    center = jnp.where(left, shifted, couplings[0])
    square, tall, thin, full = (order, width), (order + rhs, width), (rhs, width), (width, width)

    new_v, new_u, cross, kept_v, kept_b, kept_u = call(
        interior_kernel,
        [tall, tall, square, square, thin, square],
        [square, full, full],
        diag, couplings[1], outer, sources,
    )
    levels = half.bit_length() - 1
    stored = []
    for level in range(levels):
        distance = 2**level
        firsts = range(distance - 1, half, 2 * distance)
        pairs = [
            (a, b) for first in firsts for a, b in zip(at(first), at(first + distance), strict=True)
        ]
        first_v = lax.ppermute(new_v, "slab", pairs)
        if level == levels - 1:
            new_v, level_v, level_b = call(
                level_kernel, [tall, square, thin], [square], new_v, new_u, cross, first_v
            )
            stored.append((distance, pairs, (level_v, level_b)))
        else:
            first_u = lax.ppermute(new_u, "slab", pairs)
            first_cross = lax.ppermute(cross, "slab", pairs)
            new_v, new_u, cross, level_v, level_b, level_u = call(
                wide_level_kernel,
                [tall, tall, square, square, thin, square],
                [square],
                new_v, new_u, cross, first_v, first_u, first_cross,
            )
            stored.append((distance, pairs, (level_v, level_b, level_u)))
    other = lax.ppermute(new_v, "slab", [(half - 1, half), (half, half - 1)])
    (value_v,) = call(center_kernel, [thin], [square, full], new_v, other, center)
    value_u = jnp.zeros_like(value_v)
    for distance, pairs, kept in reversed(stored):
        if len(kept) == 2:
            (middle,) = call(narrow_back_kernel, [thin], [], value_v, *kept)
        else:
            (middle,) = call(back_kernel, [thin], [], value_v, value_u, *kept)
        sent = lax.ppermute(
            jnp.concatenate([middle, value_u]), "slab", [(b, a) for a, b in pairs]
        )
        is_first = place % (2 * distance) == distance - 1
        value_v = jnp.where(is_first, sent[:rhs], value_v)
        value_u = jnp.where(is_first, sent[rhs:], middle)
    (result,) = call(
        final_kernel, [sources.shape], [], value_v, value_u, kept_v, kept_b, kept_u
    )
    return result


def solution(mesh):
    placed = (
        P(("energy", "slab"), "orb", None),
        P(("energy", "slab"), None, None),
        P(("energy", "slab"), ("orb", "rhs"), None),
    )
    return jax.shard_map(
        local,
        mesh=mesh,
        in_specs=placed,
        out_specs=P(("energy", "slab"), ("orb", "rhs"), None),
        check_vma=False,
    )
```

time: 552 us -> 121 us (0.22); the launches traced: 541 us -> 120 us
  other arithmetic: 364 us -> 0.09 us
  Pallas kernels: 0 us -> 82.6 us
  local copies, waits for them, and re-layouts: 50.3 us -> 1.77 us
  matrix products: 46.1 us -> 0 us
  blocking collectives: 25.1 us -> 0 us
  between operations: 9.34 us -> 0.15 us
  waiting for transfers between devices: 31.5 us -> 23.1 us
    another operation x55 -> x0, other arithmetic: 355 us -> none  [the longest x22 117 us: local(): factor = jnp.linalg.cholesky(embed(pivot_whole))]
    pallas_call x0 -> x5, Pallas kernels: none -> 82.6 us  [call(): pl.pallas_call(kernel, out_shape=[jax.ShapeDtypeStruct(shape, jnp.float32...]
    another operation x101 -> x0, matrix products: 31.9 us -> none  [the longest x70 16.7 us: apply_inverse(): return jax.scipy.linalg.cho_solve((factor, True), rows.T).T]
    another operation x53 -> x0, local copies, waits for them, and re-layouts: 30.4 us -> none  [the longest x32 23.3 us: apply_inverse(): return jax.scipy.linalg.cho_solve((factor, True), rows.T).T]
    all_gather x4 -> x0, blocking collectives: 25.1 us -> none  [the longest x1 7.47 us: local(): pivot_whole = lax.all_gather(pivot_local, 'orb', axis=0, tiled=True)]
    dot_general x18 -> x0, matrix products: 14.2 us -> none  [the longest x8 5.55 us: times_flipped(): lax.dot_general(left, right, (((1,), (1,)), ((), ())), precision=lax.Prec...]
    unnamed x127 -> x6, local copies, waits for them, and re-layouts: 13.4 us -> 0.67 us
    ppermute x10 -> x5, waiting for transfers between devices: 31.5 us -> 23.1 us  [the longest x1 12.3 us: local(): lax.ppermute(jnp.concatenate([middle, value_u]), 'slab', [(b, a) for a, b...]
  transfers between devices with their start and end apart: 10 -> 5, of which waited for: 3 -> 3; matrix products, arithmetic and copies ran while one was open for 39% -> 1% of each run, Pallas kernels for 0% -> 0%
where the time goes in v1:
time: 121 us; the launch traced here: 120 us
  Pallas kernels  82.6 us (68%)
  waiting for transfers between devices  23.1 us (19%)
  starting transfers between devices  12.7 us (10%)
  local copies, waits for them, and re-layouts  1.77 us (1%)
    pallas_call x5, Pallas kernels, call(): pl.pallas_call(kernel, out_shape=[jax.ShapeDtypeStruct(shape, jnp.float32...  82.6 us
    ppermute x1, waiting for transfers between devices, local(): lax.ppermute(jnp.concatenate([middle, value_u]), 'slab', [(b, a) for a, b...  12.3 us
    ppermute x1, starting transfers between devices, local(): first_v = lax.ppermute(new_v, 'slab', pairs)  6.94 us
    ppermute x1, waiting for transfers between devices, gather_columns(): lax.ppermute(shard, 'orb', [(i, i ^ distance) for i in range(size)])  5.48 us
    ppermute x1, waiting for transfers between devices, local(): first_v = lax.ppermute(new_v, 'slab', pairs)  5.36 us
    ppermute x1, starting transfers between devices, gather_columns(): lax.ppermute(shard, 'orb', [(i, i ^ distance) for i in range(size)])  2.97 us
  transfers between devices with their start and end apart: 5, of which 3 were waited for; matrix products, arithmetic and copies ran while one was open for 1% of the time, Pallas kernels for 0%

profile of v1, /device:TPU:0, one launch (start us, length us, event | category | flops | bytes accessed | tf_op | source)
XLA Modules:
  0.0 120.4 jit_solution(12000356131135458636)
XLA Ops:
  0.0 0.0 copy-start.2
  0.0 3.0 %collective-permute-start = (f32[2,96,384]{2,1,0:T(8,128)}, f32[2,96,384]{2,1,0:T(8,128)S(1)}, u32[]{:S(2)}, u32[]{:S(2)}) collective-permute-start(f32[2,96,384]{2,1,0:T(8,128)} %param.3), channel_id=1, source_target_pairs={{0,2},{2,0},{1,3},{3,1},{4,6},{6,4},{5,7},{7,5},{8,10},{10,8},{9,1... | collective-permute-start | bytes 884744 | tf_op jit(solution)/shard_map/ppermute | solution.py:283
  3.0 1.1 slice_bitcast_fusion
  4.1 0.7 collective-permute-start.1
  4.8 0.0 copy-start.1
  4.8 5.5 %collective-permute-done = f32[2,96,384]{2,1,0:T(8,128)S(1)} collective-permute-done((f32[2,96,384]{2,1,0:T(8,128)}, f32[2,96,384]{2,1,0:T(8,128)S(1)}, u32[]{:S(2)}, u32[]{:S(2)}) %collective-permute-start) | collective-permute-done | bytes 294944 | tf_op jit(solution)/shard_map/ppermute | solution.py:283
  10.3 0.0 copy-done.2
  10.3 0.0 copy-start
  10.3 0.0 collective-permute-done.1
  10.3 0.0 copy-done.1
  10.4 0.7 copy-done
  11.0 22.4 %shard_map.37 = (f32[200,384]{1,0:T(8,128)S(1)}, f32[200,384]{1,0:T(8,128)S(1)}, f32[192,384]{1,0:T(8,128)S(1)}, f32[192,384]{1,0:T(8,128)S(1)}, f32[8,384]{1,0:T(8,128)S(1)}, /*index=5*/f32[192,384]{1,0:T(8,128)S(1)}) custom-call(f32[2,192,384]{2,1,0:T(8,128)S(1)} %maximum_select_fusion.diag, f32[192,384]{1,0:T(8,128)S(1)} %get-tuple-element.26.inner, ...), custom_call_target="tpu_custom_call" | custom-call | tf_op jit(solution)/shard_map/pallas_call | solution.py:270
  33.4 6.9 %collective-permute-start.2 = (f32[200,384]{1,0:T(8,128)S(1)}, f32[200,384]{1,0:T(8,128)S(1)}, u32[]{:S(2)}, u32[]{:S(2)}) collective-permute-start(f32[200,384]{1,0:T(8,128)S(1)} %get-tuple-element.14.own_v), channel_id=1, source_target_pairs={{0,4},{12,8},{1,5},{13,9},{2,6},{14,10},{3,7},{15,11},{16,20},{28,... | collective-permute-start | bytes 921608 | tf_op jit(solution)/shard_map/ppermute | solution.py:326
  40.4 5.4 %collective-permute-done.2.first_v = f32[200,384]{1,0:T(8,128)S(1)} collective-permute-done((f32[200,384]{1,0:T(8,128)S(1)}, f32[200,384]{1,0:T(8,128)S(1)}, u32[]{:S(2)}, u32[]{:S(2)}) %collective-permute-start.2) | collective-permute-done | bytes 307232 | tf_op jit(solution)/shard_map/ppermute | solution.py:326
  45.7 19.8 %shard_map.38 = (f32[200,384]{1,0:T(8,128)S(1)}, f32[192,384]{1,0:T(8,128)S(1)}, f32[8,384]{1,0:T(8,128)S(1)}) custom-call(f32[200,384]{1,0:T(8,128)S(1)} %get-tuple-element.14.own_v, f32[200,384]{1,0:T(8,128)S(1)} %get-tuple-element.15.own_u, f32[192,384]{1,0:T(8,128)S(1)} %get-tuple-element.16.own_cross, f32[200,384]{1,0:T(8,128)S(1)} %collective-permute-done.2.first_v), custom_call_target="tpu_custom_call" | custom-call | tf_op jit(solution)/shard_map/pallas_call | solution.py:270
  65.6 0.9 collective-permute-start.3
  66.4 0.0 collective-permute-done.3.other
  66.4 38.5 %shard_map.39.value_v = f32[8,384]{1,0:T(8,128)S(1)} custom-call(f32[200,384]{1,0:T(8,128)S(1)} %get-tuple-element.17.own, f32[200,384]{1,0:T(8,128)S(1)} %collective-permute-done.3.other, f32[192,384]{1,0:T(8,128)S(1)} %get-tuple-element.23.coupling), custom_call_target="tpu_custom_call" | custom-call | tf_op jit(solution)/shard_map/pallas_call | solution.py:270
  104.9 0.5 shard_map.40
  105.4 1.3 %collective-permute-start.4 = (f32[16,384]{1,0:T(8,128)S(1)}, f32[16,384]{1,0:T(8,128)S(1)}, u32[]{:S(2)}, u32[]{:S(2)}) collective-permute-start(f32[16,384]{1,0:T(8,128)S(1)} %concatenate.11), channel_id=1, source_target_pairs={{4,0},{8,12},{5,1},{9,13},{6,2},{10,14},{7,3},{11,15},{20,16},{24,... | collective-permute-start | bytes 73736 | tf_op jit(solution)/shard_map/ppermute | solution.py:350
  106.7 12.3 %collective-permute-done.4 = f32[16,384]{1,0:T(8,128)S(1)} collective-permute-done((f32[16,384]{1,0:T(8,128)S(1)}, f32[16,384]{1,0:T(8,128)S(1)}, u32[]{:S(2)}, u32[]{:S(2)}) %collective-permute-start.4) | collective-permute-done | bytes 24608 | tf_op jit(solution)/shard_map/ppermute | solution.py:350
  119.0 1.4 %shard_map.41 = f32[2,8,384]{2,1,0:T(8,128)} custom-call(f32[8,384]{1,0:T(8,128)S(1)} %get-tuple-element.28.value_v, f32[8,384]{1,0:T(8,128)S(1)} %get-tuple-element.27.value_u, f32[192,384]{1,0:T(8,128)S(1)} %get-tuple-element.20.kept_v, f32[8,384]{1,0:T(8,128)S(1)} %get-tuple-element.21.kept_b, f32[192,384]{1,0:T(8,128)S(1)} %get-tuple-element.22.kept_u), custom_call_target="tpu_custom_call" | custom-call | tf_op jit(solution)/shard_map/pallas_call | solution.py:270
  (4 shorter events, 0.1 us)
Async XLA Ops:
  0.0 10.3 %copy-start.2 = (f32[2,96,384]{2,1,0:T(8,128)S(1)}, f32[2,96,384]{2,1,0:T(8,128)}, u32[]{:S(2)}) copy-start(f32[2,96,384]{2,1,0:T(8,128)} %param.3) | copy-start | bytes 884740
  0.0 10.3 %collective-permute-start = (f32[2,96,384]{2,1,0:T(8,128)}, f32[2,96,384]{2,1,0:T(8,128)S(1)}, u32[]{:S(2)}, u32[]{:S(2)}) collective-permute-start(f32[2,96,384]{2,1,0:T(8,128)} %param.3), channel_id=1, source_target_pairs={{0,2},{2,0},{1,3},{3,1},{4,6},{6,4},{5,7},{7,5},{8,10},{10,8},{9,1... | collective-permute-start | bytes 884744 | tf_op jit(solution)/shard_map/ppermute | solution.py:283
  4.1 6.3 %collective-permute-start.1 = (f32[192,384]{1,0:T(8,128)S(1)}, f32[192,384]{1,0:T(8,128)S(1)}, u32[]{:S(2)}, u32[]{:S(2)}) collective-permute-start(f32[192,384]{1,0:T(8,128)S(1)} %get-tuple-element.25), channel_id=1, source_target_pairs={{8,4},{12,8},{9,5},{13,9},{10,6},{14,10},{11,7},{15,11},{24,20},{2... | collective-permute-start | bytes 884744 | tf_op jit(solution)/shard_map/ppermute | solution.py:306
  4.8 5.6 %copy-start.1 = (f32[2,192,384]{2,1,0:T(8,128)S(1)}, f32[2,192,384]{2,1,0:T(8,128)}, u32[]{:S(2)}) copy-start(f32[2,192,384]{2,1,0:T(8,128)} %param.4) | copy-start | bytes 1769476
  10.3 0.7 copy-start
  33.4 12.3 %collective-permute-start.2 = (f32[200,384]{1,0:T(8,128)S(1)}, f32[200,384]{1,0:T(8,128)S(1)}, u32[]{:S(2)}, u32[]{:S(2)}) collective-permute-start(f32[200,384]{1,0:T(8,128)S(1)} %get-tuple-element.14.own_v), channel_id=1, source_target_pairs={{0,4},{12,8},{1,5},{13,9},{2,6},{14,10},{3,7},{15,11},{16,20},{28,... | collective-permute-start | bytes 921608 | tf_op jit(solution)/shard_map/ppermute | solution.py:326
  65.6 0.9 collective-permute-start.3
  105.4 13.6 %collective-permute-start.4 = (f32[16,384]{1,0:T(8,128)S(1)}, f32[16,384]{1,0:T(8,128)S(1)}, u32[]{:S(2)}, u32[]{:S(2)}) collective-permute-start(f32[16,384]{1,0:T(8,128)S(1)} %concatenate.11), channel_id=1, source_target_pairs={{4,0},{8,12},{5,1},{9,13},{6,2},{10,14},{7,3},{11,15},{20,16},{24,... | collective-permute-start | bytes 73736 | tf_op jit(solution)/shard_map/ppermute | solution.py:350

commit v2 on v1

--- a/solution.py
+++ b/solution.py
@@ -67,67 +67,186 @@
     )
 
 
-GROUP = 8
+GROUP = 16
+TALL = 8
+
+
+def product(left, right):
+    return (left[0] * right[0] - left[1] * right[1], left[0] * right[1] + left[1] * right[0])
+
+
+def conjugate(value):
+    return (value[0], -value[1])
+
+
+def plus(left, right):
+    return (left[0] + right[0], left[1] + right[1])
+
+
+def minus(left, right):
+    return (left[0] - right[0], left[1] - right[1])
+
+
+def squared(value):
+    return value[0] * value[0] + value[1] * value[1]
+
+
+def scaled_by(value, factor):
+    return (value[0] * factor, value[1] * factor)
+
+
+def invert_pair(head, cross, tail):
+    scale = 1.0 / (head * tail - squared(cross))
+    return tail * scale, scaled_by(cross, -scale), head * scale
+
+
+def invert_four(at):
+    head = invert_pair(at[0][0][0], at[0][1], at[1][1][0])
+    upper = [[at[0][2], at[0][3]], [at[1][2], at[1][3]]]
+    mixed = [
+        [plus(scaled_by(upper[0][j], head[0]), product(head[1], upper[1][j])) for j in range(2)],
+        [
+            plus(product(conjugate(head[1]), upper[0][j]), scaled_by(upper[1][j], head[2]))
+            for j in range(2)
+        ],
+    ]
+
+    def schur(i, j):
+        return plus(
+            product(conjugate(upper[0][i]), mixed[0][j]),
+            product(conjugate(upper[1][i]), mixed[1][j]),
+        )
+
+    tail = invert_pair(
+        at[2][2][0] - schur(0, 0)[0],
+        minus(at[2][3], schur(0, 1)),
+        at[3][3][0] - schur(1, 1)[0],
+    )
+    carried = [
+        [
+            plus(scaled_by(mixed[i][0], tail[0]), product(mixed[i][1], conjugate(tail[1]))),
+            plus(product(mixed[i][0], tail[1]), scaled_by(mixed[i][1], tail[2])),
+        ]
+        for i in range(2)
+    ]
+
+    def corner(i, j):
+        return plus(
+            product(carried[i][0], conjugate(mixed[j][0])),
+            product(carried[i][1], conjugate(mixed[j][1])),
+        )
+
+    zero = jnp.zeros_like(head[0])
+    result = [[None] * 4 for _ in range(4)]
+    result[0][0] = (head[0] + corner(0, 0)[0], zero)
+    result[0][1] = plus(head[1], corner(0, 1))
+    result[1][1] = (head[2] + corner(1, 1)[0], zero)
+    result[2][2], result[2][3], result[3][3] = (tail[0], zero), tail[1], (tail[2], zero)
+    for i in range(2):
+        for j in range(2):
+            result[i][2 + j] = (-carried[i][j][0], -carried[i][j][1])
+    for i in range(4):
+        for j in range(i):
+            result[i][j] = conjugate(result[j][i])
+    return result
+
+
+def spread_row(rows, at):
+    return jnp.broadcast_to(rows[at : at + 1], (TALL, LANES))
+
+
+def spread_lane(rows, at):
+    return jnp.broadcast_to(rows[:, at : at + 1], (TALL, LANES))
 
 
 def invert_group(rows, first, sign, lane, row_id):
-    for offset in range(0, GROUP, 2):
+    parts = [rows[start : start + TALL] for start in range(0, GROUP, TALL)]
+    for offset in range(0, GROUP, 4):
         step = first + offset
-        at_zero = lane == step
-        at_one = lane == step + 1
-        at_any = at_zero | at_one | (lane == step + HALF) | (lane == step + 1 + HALF)
-        zero_real, zero_imag, one_real, one_imag = (
-            jnp.broadcast_to(rows[:, at : at + 1], (GROUP, LANES))
-            for at in (step, step + HALF, step + 1, step + 1 + HALF)
-        )
-        head = zero_real[offset : offset + 1]
-        tail = one_real[offset + 1 : offset + 2]
-        cross_real = one_real[offset : offset + 1]
-        cross_imag = one_imag[offset : offset + 1]
-        scale = 1.0 / (head * tail - cross_real * cross_real - cross_imag * cross_imag)
-        cleared = jnp.where(at_any, 0.0, rows)
+        home, inner = divmod(offset, TALL)
+        columns = [
+            [(spread_lane(part, step + at), spread_lane(part, step + at + HALF)) for at in range(4)]
+            for part in parts
+        ]
+        inverse = invert_four(
+            [
+                [
+                    tuple(spread_row(value, inner + i) for value in columns[home][j])
+                    if j >= i
+                    else None
+                    for j in range(4)
+                ]
+                for i in range(4)
+            ]
+        )
+        inside = (lane % HALF >= step) & (lane % HALF < step + 4)
+        cleared = jnp.where(inside, 0.0, parts[home])
         turned = pltpu.roll(cleared, HALF, 1) * sign
-        row_zero = cleared[offset : offset + 1] + jnp.where(at_zero, 1.0, 0.0)
-        row_one = cleared[offset + 1 : offset + 2] + jnp.where(at_one, 1.0, 0.0)
-        turn_zero = turned[offset : offset + 1] + jnp.where(lane == step + HALF, 1.0, 0.0)
-        turn_one = turned[offset + 1 : offset + 2] + jnp.where(lane == step + 1 + HALF, 1.0, 0.0)
-        new_zero = (tail * row_zero - cross_real * row_one - cross_imag * turn_one) * scale
-        new_one = (head * row_one - cross_real * row_zero + cross_imag * turn_zero) * scale
-        spin_zero = (tail * turn_zero - cross_real * turn_one + cross_imag * row_one) * scale
-        spin_one = (head * turn_one - cross_real * turn_zero - cross_imag * row_zero) * scale
-        fresh = (
-            cleared
-            - (zero_real * new_zero + zero_imag * spin_zero)
-            - (one_real * new_one + one_imag * spin_one)
-        )
-        rows = jnp.where(
-            row_id == offset, new_zero, jnp.where(row_id == offset + 1, new_one, fresh)
-        )
-    return rows
+        plain, spun = [], []
+        for at in range(4):
+            plain.append(spread_row(cleared, inner + at) + jnp.where(lane == step + at, 1.0, 0.0))
+            spun.append(
+                spread_row(turned, inner + at) + jnp.where(lane == step + at + HALF, 1.0, 0.0)
+            )
+        new_rows, new_spins = [], []
+        for i in range(4):
+            new = spin = None
+            for j in range(4):
+                real, imag = inverse[i][j]
+                if i == j:
+                    term, turn = real * plain[j], real * spun[j]
+                else:
+                    term = real * plain[j] + imag * spun[j]
+                    turn = real * spun[j] - imag * plain[j]
+                new, spin = (term, turn) if new is None else (new + term, spin + turn)
+            new_rows.append(new)
+            new_spins.append(spin)
+        updated = []
+        for index, part in enumerate(parts):
+            fresh = jnp.where(inside, 0.0, part)
+            for i in range(4):
+                real, imag = columns[index][i]
+                fresh = fresh - (real * new_rows[i] + imag * new_spins[i])
+            if index == home:
+                for i in range(4):
+                    fresh = jnp.where(row_id == inner + i, new_rows[i], fresh)
+            updated.append(fresh)
+        parts = updated
+    return jnp.concatenate(parts, axis=0) if len(parts) > 1 else parts[0]
+
+
+def spread_out(done, spun, first):
+    last = HALF - first - GROUP
+    before = [jnp.zeros((first, LANES), jnp.float32)] if first else []
+    after = [jnp.zeros((last, LANES), jnp.float32)] if last else []
+    return jnp.concatenate(before + [done] + after + before + [spun] + after, axis=0)
 
 
 def invert_small(block):
     lane = lax.broadcasted_iota(jnp.int32, (1, LANES), 1)
-    row_id = lax.broadcasted_iota(jnp.int32, (GROUP, 1), 0)
+    row_id = lax.broadcasted_iota(jnp.int32, (TALL, 1), 0)
     sign = lane_sign((1, LANES))
-    groups = [block[start : start + GROUP] for start in range(0, HALF, GROUP)]
-    for home in range(len(groups)):
-        first = home * GROUP
-        done = invert_group(groups[home], first, sign, lane, row_id)
+    group = block[:GROUP]
+    for first in range(0, HALF, GROUP):
+        done = invert_group(group, first, sign, lane, row_id)
         spun = pltpu.roll(done, HALF, 1) * sign
         inside = (lane % HALF >= first) & (lane % HALF < first + GROUP)
-        for index, group in enumerate(groups):
-            if index == home:
-                continue
-            fresh = jnp.where(inside, 0.0, group)
+        following = first + GROUP
+        if following < HALF:
+            old = block[following : following + GROUP]
+            group = jnp.where(inside, 0.0, old)
             for at in range(GROUP):
-                fresh = fresh - (
-                    group[:, first + at : first + at + 1] * done[at : at + 1]
-                    + group[:, first + at + HALF : first + at + HALF + 1] * spun[at : at + 1]
+                group = group - (
+                    old[:, first + at : first + at + 1] * done[at : at + 1]
+                    + old[:, first + at + HALF : first + at + HALF + 1] * spun[at : at + 1]
                 )
-            groups[index] = fresh
-        groups[home] = done
-    return jnp.concatenate(groups, axis=0)
+        rest = jnp.where(inside, 0.0, block) - dot(
+            jnp.where(inside, block, 0.0), spread_out(done, spun, first)
+        )
+        above = [rest[:first]] if first else []
+        below = [rest[following:]] if following < HALF else []
+        block = jnp.concatenate(above + [done] + below, axis=0)
+    return block
 
 
 def invert(ref):

time: 121 us -> 98.7 us (0.82)
  Pallas kernels: 82.6 us -> 60.6 us
    pallas_call x5, Pallas kernels: 82.6 us -> 60.6 us  [call(): pl.pallas_call(kernel, out_shape=[jax.ShapeDtypeStruct(shape, jnp.float32...]
where the time goes in v2:
time: 98.7 us; the launch traced here: 98.5 us
  Pallas kernels  60.6 us (61%)
  waiting for transfers between devices  23.1 us (23%)
  starting transfers between devices  12.7 us (13%)
  local copies, waits for them, and re-layouts  1.77 us (2%)
    pallas_call x5, Pallas kernels, call(): pl.pallas_call(kernel, out_shape=[jax.ShapeDtypeStruct(shape, jnp.float32...  60.6 us
    ppermute x1, waiting for transfers between devices, local(): lax.ppermute(jnp.concatenate([middle, value_u]), 'slab', [(b, a) for a, b...  12.3 us
    ppermute x1, starting transfers between devices, local(): first_v = lax.ppermute(new_v, 'slab', pairs)  6.94 us
    ppermute x1, waiting for transfers between devices, gather_columns(): lax.ppermute(shard, 'orb', [(i, i ^ distance) for i in range(size)])  5.48 us
    ppermute x1, waiting for transfers between devices, local(): first_v = lax.ppermute(new_v, 'slab', pairs)  5.36 us
    ppermute x1, starting transfers between devices, gather_columns(): lax.ppermute(shard, 'orb', [(i, i ^ distance) for i in range(size)])  2.97 us
  transfers between devices with their start and end apart: 5, of which 3 were waited for; matrix products, arithmetic and copies ran while one was open for 1% of the time, Pallas kernels for 0%

profile of v2, /device:TPU:0, one launch (start us, length us, event | category | flops | bytes accessed | tf_op | source)
XLA Modules:
  0.0 98.5 jit_solution(17674766720712771484)
XLA Ops:
  0.0 0.0 copy-start.2
  0.0 3.0 %collective-permute-start = (f32[2,96,384]{2,1,0:T(8,128)}, f32[2,96,384]{2,1,0:T(8,128)S(1)}, u32[]{:S(2)}, u32[]{:S(2)}) collective-permute-start(f32[2,96,384]{2,1,0:T(8,128)} %param.3), channel_id=1, source_target_pairs={{0,2},{2,0},{1,3},{3,1},{4,6},{6,4},{5,7},{7,5},{8,10},{10,8},{9,1... | collective-permute-start | bytes 884744 | tf_op jit(solution)/shard_map/ppermute | solution.py:402
  3.0 1.1 %slice_bitcast_fusion = (f32[192,384]{1,0:T(8,128)S(1)}, f32[192,384]{1,0:T(8,128)S(1)}) fusion(f32[2,192,384]{2,1,0:T(8,128)} %param.4), kind=kLoop, calls=%fused_computation.2 | loop fusion | bytes 1179648 | tf_op jit(solution)/shard_map/squeeze | solution.py:427
  4.1 0.7 collective-permute-start.1
  4.8 0.0 copy-start.1
  4.8 5.5 %collective-permute-done = f32[2,96,384]{2,1,0:T(8,128)S(1)} collective-permute-done((f32[2,96,384]{2,1,0:T(8,128)}, f32[2,96,384]{2,1,0:T(8,128)S(1)}, u32[]{:S(2)}, u32[]{:S(2)}) %collective-permute-start) | collective-permute-done | bytes 294944 | tf_op jit(solution)/shard_map/ppermute | solution.py:402
  10.3 0.0 copy-done.2
  10.3 0.0 copy-start
  10.3 0.0 collective-permute-done.1
  10.3 0.0 copy-done.1
  10.4 0.7 copy-done
  11.0 16.9 %shard_map.37 = (f32[200,384]{1,0:T(8,128)S(1)}, f32[200,384]{1,0:T(8,128)S(1)}, f32[192,384]{1,0:T(8,128)S(1)}, f32[192,384]{1,0:T(8,128)S(1)}, f32[8,384]{1,0:T(8,128)S(1)}, /*index=5*/f32[192,384]{1,0:T(8,128)S(1)}) custom-call(f32[2,192,384]{2,1,0:T(8,128)S(1)} %maximum_select_fusion.diag, f32[192,384]{1,0:T(8,128)S(1)} %get-tuple-element.26.inner, ...), custom_call_target="tpu_custom_call" | custom-call | tf_op jit(solution)/shard_map/pallas_call | solution.py:389
  27.9 6.9 %collective-permute-start.2 = (f32[200,384]{1,0:T(8,128)S(1)}, f32[200,384]{1,0:T(8,128)S(1)}, u32[]{:S(2)}, u32[]{:S(2)}) collective-permute-start(f32[200,384]{1,0:T(8,128)S(1)} %get-tuple-element.14.own_v), channel_id=1, source_target_pairs={{0,4},{12,8},{1,5},{13,9},{2,6},{14,10},{3,7},{15,11},{16,20},{28,... | collective-permute-start | bytes 921608 | tf_op jit(solution)/shard_map/ppermute | solution.py:445
  34.9 5.4 %collective-permute-done.2.first_v = f32[200,384]{1,0:T(8,128)S(1)} collective-permute-done((f32[200,384]{1,0:T(8,128)S(1)}, f32[200,384]{1,0:T(8,128)S(1)}, u32[]{:S(2)}, u32[]{:S(2)}) %collective-permute-start.2) | collective-permute-done | bytes 307232 | tf_op jit(solution)/shard_map/ppermute | solution.py:445
  40.2 14.4 %shard_map.38 = (f32[200,384]{1,0:T(8,128)S(1)}, f32[192,384]{1,0:T(8,128)S(1)}, f32[8,384]{1,0:T(8,128)S(1)}) custom-call(f32[200,384]{1,0:T(8,128)S(1)} %get-tuple-element.14.own_v, f32[200,384]{1,0:T(8,128)S(1)} %get-tuple-element.15.own_u, f32[192,384]{1,0:T(8,128)S(1)} %get-tuple-element.16.own_cross, f32[200,384]{1,0:T(8,128)S(1)} %collective-permute-done.2.first_v), custom_call_target="tpu_custom_call" | custom-call | tf_op jit(solution)/shard_map/pallas_call | solution.py:389
  54.6 0.9 collective-permute-start.3
  55.5 0.0 collective-permute-done.3.other
  55.5 27.5 %shard_map.39.value_v = f32[8,384]{1,0:T(8,128)S(1)} custom-call(f32[200,384]{1,0:T(8,128)S(1)} %get-tuple-element.17.own, f32[200,384]{1,0:T(8,128)S(1)} %collective-permute-done.3.other, f32[192,384]{1,0:T(8,128)S(1)} %get-tuple-element.23.coupling), custom_call_target="tpu_custom_call" | custom-call | tf_op jit(solution)/shard_map/pallas_call | solution.py:389
  83.0 0.5 shard_map.40
  83.5 1.3 %collective-permute-start.4 = (f32[16,384]{1,0:T(8,128)S(1)}, f32[16,384]{1,0:T(8,128)S(1)}, u32[]{:S(2)}, u32[]{:S(2)}) collective-permute-start(f32[16,384]{1,0:T(8,128)S(1)} %concatenate.11), channel_id=1, source_target_pairs={{4,0},{8,12},{5,1},{9,13},{6,2},{10,14},{7,3},{11,15},{20,16},{24,... | collective-permute-start | bytes 73736 | tf_op jit(solution)/shard_map/ppermute | solution.py:469
  84.8 12.3 %collective-permute-done.4 = f32[16,384]{1,0:T(8,128)S(1)} collective-permute-done((f32[16,384]{1,0:T(8,128)S(1)}, f32[16,384]{1,0:T(8,128)S(1)}, u32[]{:S(2)}, u32[]{:S(2)}) %collective-permute-start.4) | collective-permute-done | bytes 24608 | tf_op jit(solution)/shard_map/ppermute | solution.py:469
  97.1 1.4 %shard_map.41 = f32[2,8,384]{2,1,0:T(8,128)} custom-call(f32[8,384]{1,0:T(8,128)S(1)} %get-tuple-element.28.value_v, f32[8,384]{1,0:T(8,128)S(1)} %get-tuple-element.27.value_u, f32[192,384]{1,0:T(8,128)S(1)} %get-tuple-element.20.kept_v, f32[8,384]{1,0:T(8,128)S(1)} %get-tuple-element.21.kept_b, f32[192,384]{1,0:T(8,128)S(1)} %get-tuple-element.22.kept_u), custom_call_target="tpu_custom_call" | custom-call | tf_op jit(solution)/shard_map/pallas_call | solution.py:389
  (4 shorter events, 0.1 us)
Async XLA Ops:
  0.0 10.3 %copy-start.2 = (f32[2,96,384]{2,1,0:T(8,128)S(1)}, f32[2,96,384]{2,1,0:T(8,128)}, u32[]{:S(2)}) copy-start(f32[2,96,384]{2,1,0:T(8,128)} %param.3) | copy-start | bytes 884740
  0.0 10.3 %collective-permute-start = (f32[2,96,384]{2,1,0:T(8,128)}, f32[2,96,384]{2,1,0:T(8,128)S(1)}, u32[]{:S(2)}, u32[]{:S(2)}) collective-permute-start(f32[2,96,384]{2,1,0:T(8,128)} %param.3), channel_id=1, source_target_pairs={{0,2},{2,0},{1,3},{3,1},{4,6},{6,4},{5,7},{7,5},{8,10},{10,8},{9,1... | collective-permute-start | bytes 884744 | tf_op jit(solution)/shard_map/ppermute | solution.py:402
  4.1 6.3 %collective-permute-start.1 = (f32[192,384]{1,0:T(8,128)S(1)}, f32[192,384]{1,0:T(8,128)S(1)}, u32[]{:S(2)}, u32[]{:S(2)}) collective-permute-start(f32[192,384]{1,0:T(8,128)S(1)} %get-tuple-element.25), channel_id=1, source_target_pairs={{8,4},{12,8},{9,5},{13,9},{10,6},{14,10},{11,7},{15,11},{24,20},{2... | collective-permute-start | bytes 884744 | tf_op jit(solution)/shard_map/ppermute | solution.py:425
  4.8 5.6 %copy-start.1 = (f32[2,192,384]{2,1,0:T(8,128)S(1)}, f32[2,192,384]{2,1,0:T(8,128)}, u32[]{:S(2)}) copy-start(f32[2,192,384]{2,1,0:T(8,128)} %param.4) | copy-start | bytes 1769476
  10.3 0.7 copy-start
  27.9 12.3 %collective-permute-start.2 = (f32[200,384]{1,0:T(8,128)S(1)}, f32[200,384]{1,0:T(8,128)S(1)}, u32[]{:S(2)}, u32[]{:S(2)}) collective-permute-start(f32[200,384]{1,0:T(8,128)S(1)} %get-tuple-element.14.own_v), channel_id=1, source_target_pairs={{0,4},{12,8},{1,5},{13,9},{2,6},{14,10},{3,7},{15,11},{16,20},{28,... | collective-permute-start | bytes 921608 | tf_op jit(solution)/shard_map/ppermute | solution.py:445
  54.6 0.9 collective-permute-start.3
  83.5 13.6 %collective-permute-start.4 = (f32[16,384]{1,0:T(8,128)S(1)}, f32[16,384]{1,0:T(8,128)S(1)}, u32[]{:S(2)}, u32[]{:S(2)}) collective-permute-start(f32[16,384]{1,0:T(8,128)S(1)} %concatenate.11), channel_id=1, source_target_pairs={{4,0},{8,12},{5,1},{9,13},{6,2},{10,14},{7,3},{11,15},{20,16},{24,... | collective-permute-start | bytes 73736 | tf_op jit(solution)/shard_map/ppermute | solution.py:469

commit v3 on v2

--- a/solution.py
+++ b/solution.py
@@ -270,8 +270,14 @@
 
 
 def eliminate(pivot_ref, to_pivot_v, to_pivot_u, block_v, block_u, load_i, load_v, load_u):
+    invert(pivot_ref)
+    return apply_pivot(
+        pivot_ref, to_pivot_v, to_pivot_u, block_v, block_u, load_i, load_v, load_u
+    )
+
+
+def apply_pivot(pivot_ref, to_pivot_v, to_pivot_u, block_v, block_u, load_i, load_v, load_u):
     order, rhs = block_v.shape[0], load_i.shape[0]
-    invert(pivot_ref)
     inverse = embed(pivot_ref[...])
     stacked = [compact(to_pivot_v), load_i]
     if to_pivot_u is not None:
@@ -303,19 +309,25 @@
     return lax.axis_index("slab") < lax.axis_size("slab") // 2
 
 
-def interior_kernel(diag, inner, outer, loads, new_v, new_u, cross, kept_v, kept_b, kept_u, pivot, to_v, to_u):
+def invert_kernel(block, inverse):
+    inverse[...] = interleave(block[...])
+    invert(inverse)
+
+
+def interior_kernel(
+    inverse, boundary, inner, outer, loads,
+    new_v, new_u, cross, kept_v, kept_b, kept_u, to_v, to_u,
+):
     left = is_left()
-    order = diag.shape[1]
     at_interior = jnp.where(left, 0, 1)
     flip_where(left, to_v, embed(interleave(inner[...])))
     flip_where(jnp.logical_not(left), to_u, embed(interleave(outer[...])))
-    pivot[...] = interleave(diag[at_interior])
     load_i = interleave(loads[at_interior])
     load_v = interleave(loads[1 - at_interior])
-    block_v = interleave(diag[1 - at_interior])
+    block_v = interleave(boundary[...])
     zero = jnp.zeros_like(block_v)
-    new_v[...], new_u[...], cross[...], kept = eliminate(
-        pivot, to_v[...], to_u[...], block_v, zero, load_i, load_v, jnp.zeros_like(load_v)
+    new_v[...], new_u[...], cross[...], kept = apply_pivot(
+        inverse, to_v[...], to_u[...], block_v, zero, load_i, load_v, jnp.zeros_like(load_v)
     )
     kept_v[...], kept_b[...], kept_u[...] = kept
 
@@ -385,11 +397,14 @@
     result[1 - at_interior] = separate(value_v[...])
 
 
-def call(kernel, outs, scratch, *operands):
+def call(kernel, outs, scratch, *operands, flops=0):
     return pl.pallas_call(
         kernel,
         out_shape=[jax.ShapeDtypeStruct(shape, jnp.float32) for shape in outs],
         scratch_shapes=[pltpu.VMEM(shape, jnp.float32) for shape in scratch],
+        cost_estimate=pl.CostEstimate(flops=flops, bytes_accessed=flops // 64, transcendentals=0)
+        if flops
+        else None,
         compiler_params=pltpu.CompilerParams(vmem_limit_bytes=48 * 1024 * 1024),
     )(*operands)
 
@@ -403,8 +418,8 @@
         first = index // distance % 2 == 0
         shard = jnp.where(
             first,
-            jnp.concatenate([shard, theirs], axis=1),
-            jnp.concatenate([theirs, shard], axis=1),
+            jnp.concatenate([shard, theirs], axis=0),
+            jnp.concatenate([theirs, shard], axis=0),
         )
         distance *= 2
     return shard
@@ -423,16 +438,20 @@
         return (position, slabs - 1 - position)
 
     shifted = lax.ppermute(couplings[0], "slab", [(i, i - 1) for i in range(half, slabs)])
-    diag = gather_columns(diag_blocks)
+    interior = gather_columns(jnp.where(left, diag_blocks[0], diag_blocks[1]))
+    held = jnp.where(left, diag_blocks[1], diag_blocks[0])
+    interior, held = lax.optimization_barrier((interior, held))
+    boundary = gather_columns(held)
     outer = jnp.where(left, jnp.where(slab > 0, couplings[0], 0.0), shifted)
     center = jnp.where(left, shifted, couplings[0])
     square, tall, thin, full = (order, width), (order + rhs, width), (rhs, width), (width, width)
 
+    (inverse,) = call(invert_kernel, [square], [], interior, flops=64 * order * width * width)
     new_v, new_u, cross, kept_v, kept_b, kept_u = call(
         interior_kernel,
         [tall, tall, square, square, thin, square],
-        [square, full, full],
-        diag, couplings[1], outer, sources,
+        [full, full],
+        inverse, boundary, couplings[1], outer, sources,
     )
     levels = half.bit_length() - 1
     stored = []

time: 98.7 us -> 94.9 us (0.961)
  waiting for transfers between devices: 23.1 us -> 20.9 us
  starting transfers between devices: 12.7 us -> 11 us
  other arithmetic: 0.09 us -> 1.16 us
  local copies, waits for them, and re-layouts: 1.77 us -> 0.72 us
    ppermute x1, starting transfers between devices: 6.94 us -> 3.5 us  [local(): first_v = lax.ppermute(new_v, 'slab', pairs)]
    ppermute x1 -> x2, waiting for transfers between devices: 5.48 us -> 3.1 us  [gather_columns(): lax.ppermute(shard, 'orb', [(i, i ^ distance) for i in range(size)])]
    ppermute x1 -> x2, starting transfers between devices: 2.97 us -> 4.84 us  [gather_columns(): lax.ppermute(shard, 'orb', [(i, i ^ distance) for i in range(size)])]
    select_n x1 -> x3, other arithmetic: 0.04 us -> 1.11 us  [the longest x1 1.06 us: local(): held = jnp.where(left, diag_blocks[1], diag_blocks[0])]
    squeeze x1, local copies, waits for them, and re-layouts: 1.09 us -> 0.04 us  [local(): outer = jnp.where(left, jnp.where(slab > 0, couplings[0], 0.0), shifted)]
    pallas_call x5 -> x6, Pallas kernels: 60.6 us -> 60.8 us  [call(): pl.pallas_call(kernel, out_shape=[jax.ShapeDtypeStruct(shape, jnp.float32...]
  transfers between devices with their start and end apart: 5 -> 6, of which waited for: 3 -> 3; matrix products, arithmetic and copies ran while one was open for 1% -> 0% of each run, Pallas kernels for 0% -> 13%
where the time goes in v3:
time: 94.9 us; the launch traced here: 94.7 us
  Pallas kernels  60.8 us (64%)
  waiting for transfers between devices  20.9 us (22%)
  starting transfers between devices  11 us (12%)
  other arithmetic  1.16 us (1%)
    pallas_call x6, Pallas kernels, call(): pl.pallas_call(kernel, out_shape=[jax.ShapeDtypeStruct(shape, jnp.float32...  60.8 us
    ppermute x1, waiting for transfers between devices, local(): lax.ppermute(jnp.concatenate([middle, value_u]), 'slab', [(b, a) for a, b...  12.5 us
    ppermute x1, waiting for transfers between devices, local(): first_v = lax.ppermute(new_v, 'slab', pairs)  5.36 us
    ppermute x2, starting transfers between devices, gather_columns(): lax.ppermute(shard, 'orb', [(i, i ^ distance) for i in range(size)])  4.84 us
    ppermute x1, starting transfers between devices, local(): first_v = lax.ppermute(new_v, 'slab', pairs)  3.5 us
    ppermute x2, waiting for transfers between devices, gather_columns(): lax.ppermute(shard, 'orb', [(i, i ^ distance) for i in range(size)])  3.1 us
  transfers between devices with their start and end apart: 6, of which 3 were waited for; matrix products, arithmetic and copies ran while one was open for 0% of the time, Pallas kernels for 13%

profile of v3, /device:TPU:0, one launch (start us, length us, event | category | flops | bytes accessed | tf_op | source)
XLA Modules:
  0.0 94.7 jit_solution(12694490978678072926)
XLA Ops:
  0.0 0.0 copy-start.1
  0.0 1.1 %select_bitcast_fusion = (f32[96,384]{1,0:T(8,128)S(1)}, f32[96,384]{1,0:T(8,128)S(1)}) fusion(f32[2,96,384]{2,1,0:T(8,128)} %param.3, pred[]{:T(512)S(6)} %lt.15), kind=kLoop, calls=%fused_computation.5 | loop fusion | flops 73728 | bytes 589825 | tf_op jit(solution)/shard_map/jit(_where)/select_n | solution.py:442
  1.1 3.0 %collective-permute-start = (f32[96,384]{1,0:T(8,128)S(1)}, f32[96,384]{1,0:T(8,128)S(1)}, u32[]{:S(2)}, u32[]{:S(2)}) collective-permute-start(f32[96,384]{1,0:T(8,128)S(1)} %get-tuple-element.32), channel_id=1, source_target_pairs={{0,2},{2,0},{1,3},{3,1},{4,6},{6,4},{5,7},{7,5},{8,10},{10,8},{9,1... | collective-permute-start | bytes 442376 | tf_op jit(solution)/shard_map/ppermute | solution.py:417
  4.1 0.0 copy-done.1
  4.1 0.7 collective-permute-start.2
  4.9 3.1 %collective-permute-done = f32[96,384]{1,0:T(8,128)S(1)} collective-permute-done((f32[96,384]{1,0:T(8,128)S(1)}, f32[96,384]{1,0:T(8,128)S(1)}, u32[]{:S(2)}, u32[]{:S(2)}) %collective-permute-start) | collective-permute-done | bytes 147488 | tf_op jit(solution)/shard_map/ppermute | solution.py:417
  8.0 1.8 %collective-permute-start.1 = (f32[96,384]{1,0:T(8,128)S(1)}, f32[96,384]{1,0:T(8,128)S(1)}, u32[]{:S(2)}, u32[]{:S(2)}) collective-permute-start(f32[96,384]{1,0:T(8,128)S(1)} %get-tuple-element.17), channel_id=1, source_target_pairs={{0,2},{2,0},{1,3},{3,1},{4,6},{6,4},{5,7},{7,5},{8,10},{10,8},{9,1... | collective-permute-start | bytes 442376 | tf_op jit(solution)/shard_map/ppermute | solution.py:417
  9.8 12.7 %shard_map.37.inverse = f32[192,384]{1,0:T(8,128)S(1)} custom-call(f32[192,384]{1,0:T(8,128)S(1)} %maximum_select_fusion.block), custom_call_target="tpu_custom_call" | custom-call | flops 1811939328 | bytes 28311552 | tf_op jit(solution)/shard_map/pallas_call | solution.py:401
  22.5 0.0 collective-permute-done.1
  22.6 0.0 copy-start
  22.6 0.0 collective-permute-done.2
  22.6 0.7 copy-done
  23.3 4.1 %shard_map.38 = (f32[200,384]{1,0:T(8,128)S(1)}, f32[200,384]{1,0:T(8,128)S(1)}, f32[192,384]{1,0:T(8,128)S(1)}, f32[192,384]{1,0:T(8,128)S(1)}, f32[8,384]{1,0:T(8,128)S(1)}, /*index=5*/f32[192,384]{1,0:T(8,128)S(1)}) custom-call(f32[192,384]{1,0:T(8,128)S(1)} %shard_map.37.inverse, f32[192,384]{1,0:T(8,128)S(1)} %maximum_select_fusion.1.boundary, ...), custom_call_target="tpu_custom_call" | custom-call | tf_op jit(solution)/shard_map/pallas_call | solution.py:401
  27.4 3.5 %collective-permute-start.3 = (f32[200,384]{1,0:T(8,128)S(1)}, f32[200,384]{1,0:T(8,128)S(1)}, u32[]{:S(2)}, u32[]{:S(2)}) collective-permute-start(f32[200,384]{1,0:T(8,128)S(1)} %get-tuple-element.18.own_v), channel_id=1, source_target_pairs={{0,4},{12,8},{1,5},{13,9},{2,6},{14,10},{3,7},{15,11},{16,20},{28,... | collective-permute-start | bytes 921608 | tf_op jit(solution)/shard_map/ppermute | solution.py:464
  30.9 5.4 %collective-permute-done.3.first_v = f32[200,384]{1,0:T(8,128)S(1)} collective-permute-done((f32[200,384]{1,0:T(8,128)S(1)}, f32[200,384]{1,0:T(8,128)S(1)}, u32[]{:S(2)}, u32[]{:S(2)}) %collective-permute-start.3) | collective-permute-done | bytes 307232 | tf_op jit(solution)/shard_map/ppermute | solution.py:464
  36.3 14.4 %shard_map.39 = (f32[200,384]{1,0:T(8,128)S(1)}, f32[192,384]{1,0:T(8,128)S(1)}, f32[8,384]{1,0:T(8,128)S(1)}) custom-call(f32[200,384]{1,0:T(8,128)S(1)} %get-tuple-element.18.own_v, f32[200,384]{1,0:T(8,128)S(1)} %get-tuple-element.19.own_u, f32[192,384]{1,0:T(8,128)S(1)} %get-tuple-element.20.own_cross, f32[200,384]{1,0:T(8,128)S(1)} %collective-permute-done.3.first_v), custom_call_target="tpu_custom_call" | custom-call | tf_op jit(solution)/shard_map/pallas_call | solution.py:401
  50.7 0.7 collective-permute-start.4
  51.3 0.0 collective-permute-done.4.other
  51.4 27.7 %shard_map.40.value_v = f32[8,384]{1,0:T(8,128)S(1)} custom-call(f32[200,384]{1,0:T(8,128)S(1)} %get-tuple-element.21.own, f32[200,384]{1,0:T(8,128)S(1)} %collective-permute-done.4.other, f32[192,384]{1,0:T(8,128)S(1)} %get-tuple-element.27.coupling), custom_call_target="tpu_custom_call" | custom-call | tf_op jit(solution)/shard_map/pallas_call | solution.py:401
  79.0 0.5 shard_map.41
  79.5 1.3 %collective-permute-start.5 = (f32[16,384]{1,0:T(8,128)S(1)}, f32[16,384]{1,0:T(8,128)S(1)}, u32[]{:S(2)}, u32[]{:S(2)}) collective-permute-start(f32[16,384]{1,0:T(8,128)S(1)} %concatenate.19), channel_id=1, source_target_pairs={{4,0},{8,12},{5,1},{9,13},{6,2},{10,14},{7,3},{11,15},{20,16},{24,... | collective-permute-start | bytes 73736 | tf_op jit(solution)/shard_map/ppermute | solution.py:488
  80.8 12.5 %collective-permute-done.5 = f32[16,384]{1,0:T(8,128)S(1)} collective-permute-done((f32[16,384]{1,0:T(8,128)S(1)}, f32[16,384]{1,0:T(8,128)S(1)}, u32[]{:S(2)}, u32[]{:S(2)}) %collective-permute-start.5) | collective-permute-done | bytes 24608 | tf_op jit(solution)/shard_map/ppermute | solution.py:488
  93.3 1.4 %shard_map.42 = f32[2,8,384]{2,1,0:T(8,128)} custom-call(f32[8,384]{1,0:T(8,128)S(1)} %get-tuple-element.34.value_v, f32[8,384]{1,0:T(8,128)S(1)} %get-tuple-element.33.value_u, f32[192,384]{1,0:T(8,128)S(1)} %get-tuple-element.24.kept_v, f32[8,384]{1,0:T(8,128)S(1)} %get-tuple-element.25.kept_b, f32[192,384]{1,0:T(8,128)S(1)} %get-tuple-element.26.kept_u), custom_call_target="tpu_custom_call" | custom-call | tf_op jit(solution)/shard_map/pallas_call | solution.py:401
  (6 shorter events, 0.1 us)
Async XLA Ops:
  0.0 4.1 %copy-start.1 = (f32[2,192,384]{2,1,0:T(8,128)S(1)}, f32[2,192,384]{2,1,0:T(8,128)}, u32[]{:S(2)}) copy-start(f32[2,192,384]{2,1,0:T(8,128)} %param.4) | copy-start | bytes 1769476
  1.1 6.9 %collective-permute-start = (f32[96,384]{1,0:T(8,128)S(1)}, f32[96,384]{1,0:T(8,128)S(1)}, u32[]{:S(2)}, u32[]{:S(2)}) collective-permute-start(f32[96,384]{1,0:T(8,128)S(1)} %get-tuple-element.32), channel_id=1, source_target_pairs={{0,2},{2,0},{1,3},{3,1},{4,6},{6,4},{5,7},{7,5},{8,10},{10,8},{9,1... | collective-permute-start | bytes 442376 | tf_op jit(solution)/shard_map/ppermute | solution.py:417
  4.1 18.4 %collective-permute-start.2 = (f32[192,384]{1,0:T(8,128)S(1)}, f32[192,384]{1,0:T(8,128)S(1)}, u32[]{:S(2)}, u32[]{:S(2)}) collective-permute-start(f32[192,384]{1,0:T(8,128)S(1)} %get-tuple-element.29), channel_id=1, source_target_pairs={{8,4},{12,8},{9,5},{13,9},{10,6},{14,10},{11,7},{15,11},{24,20},{2... | collective-permute-start | bytes 884744 | tf_op jit(solution)/shard_map/ppermute | solution.py:440
  8.0 14.5 %collective-permute-start.1 = (f32[96,384]{1,0:T(8,128)S(1)}, f32[96,384]{1,0:T(8,128)S(1)}, u32[]{:S(2)}, u32[]{:S(2)}) collective-permute-start(f32[96,384]{1,0:T(8,128)S(1)} %get-tuple-element.17), channel_id=1, source_target_pairs={{0,2},{2,0},{1,3},{3,1},{4,6},{6,4},{5,7},{7,5},{8,10},{10,8},{9,1... | collective-permute-start | bytes 442376 | tf_op jit(solution)/shard_map/ppermute | solution.py:417
  22.6 0.7 copy-start
  27.4 8.9 %collective-permute-start.3 = (f32[200,384]{1,0:T(8,128)S(1)}, f32[200,384]{1,0:T(8,128)S(1)}, u32[]{:S(2)}, u32[]{:S(2)}) collective-permute-start(f32[200,384]{1,0:T(8,128)S(1)} %get-tuple-element.18.own_v), channel_id=1, source_target_pairs={{0,4},{12,8},{1,5},{13,9},{2,6},{14,10},{3,7},{15,11},{16,20},{28,... | collective-permute-start | bytes 921608 | tf_op jit(solution)/shard_map/ppermute | solution.py:464
  50.7 0.7 collective-permute-start.4
  79.5 13.8 %collective-permute-start.5 = (f32[16,384]{1,0:T(8,128)S(1)}, f32[16,384]{1,0:T(8,128)S(1)}, u32[]{:S(2)}, u32[]{:S(2)}) collective-permute-start(f32[16,384]{1,0:T(8,128)S(1)} %concatenate.19), channel_id=1, source_target_pairs={{4,0},{8,12},{5,1},{9,13},{6,2},{10,14},{7,3},{11,15},{20,16},{24,... | collective-permute-start | bytes 73736 | tf_op jit(solution)/shard_map/ppermute | solution.py:488
